TPU v7x, 512 devices: a whole 4x4x16 slice. The times are simulated.
512 devices in a mesh: tm: 64 (over x_lo, z, core), head: 8 (over x_hi, y).
Axes of the slice: x: 4 (x_hi: 2, x_lo: 2; x = x_hi * 2 + x_lo), y: 4, z: 16, core: 2. Of those that a mesh axis runs over, the one named last changes fastest.
Arguments:
- frames: bfloat16 [16384, 1280], P('tm', 'head'), may hold values from -6 to 6
- segment_ids: int32 [16384], replicated, may hold values from 0 to 127, never falling along the last dimension, each value on 1 to 256 neighbouring positions
- ln_gain: float32 [1280], replicated, may hold values from 0.5 to 1.5
- ln_bias: float32 [1280], replicated, may hold values from -1.5 to 1.5
- qkv_weight: bfloat16 [3, 1280, 1024], P(None, None, 'head'), may hold values from -3 to 3
- out_weight: bfloat16 [1024, 1280], P(None, 'head'), may hold values from -0.1875 to 0.1875
- out_bias: float32 [1280], P('head'), may hold values from -2.5 to 2.5
- adapter: bfloat16 [1280, 2560], P('head'), may hold values from -0.15625 to 0.15625
- rms_gain: float32 [2560], replicated, may hold values from 0.25 to 1.75
- x_weight: bfloat16 [2560, 2560], P(None, 'head'), may hold values from -0.125 to 0.125
- bc_weight: bfloat16 [2560, 256], P(None, 'head'), may hold values from -0.125 to 0.125
- decay: float32 [4096, 40], P('tm', 'head'), may hold values from 0 to 1
- skip_gain: float32 [40], P('head'), may hold values from 0.5 to 1.5
Outputs:
- encoded: bfloat16 [16384, 1280], P('tm', 'head')
- mixed: bfloat16 [4096, 2560], P('tm', 'head')
Inputs may be any that keep to these rules, and one draw needn't show every extreme that they name: `segment_ids`: segment numbers never fall along the frames; each segment holds 1 to 256 frames and one holds exactly 256.
All inputs are finite; a program needn't handle non-finite values.
Results may differ from a plain program's by a relative error of at most 0.008.
Values may be sent and summed in bfloat16 or wider, within the bound.
No kernel may reach another device: no remote copies, remote signals or barrier semaphores. Data moves between devices by JAX's collectives and lax.ppermute only.
A program may use at most 64 MiB of HBM per device.

v0:
```python
import math
import jax
import jax.numpy as jnp
from jax import lax
from jax.sharding import PartitionSpec as P

EHEAD_DIM = 64
HDIM = 64
NSTATE = 128
WINDOW = 256
EPSILON = 1e-05
HIGHEST = lax.Precision.HIGHEST


def with_halo(block, sides, width):
    for axis, dim in sides:
        count = lax.axis_size(axis)
        forward = [(i, i + 1) for i in range(count - 1)]
        backward = [(target, source) for source, target in forward]
        low = lax.ppermute(
            lax.slice_in_dim(block, block.shape[dim] - width, None, axis=dim), axis, forward
        )
        high = lax.ppermute(lax.slice_in_dim(block, 0, width, axis=dim), axis, backward)
        block = jnp.concatenate([low, block, high], axis=dim)
    return block


def prefix(part, axis, combine, identity):
    place = lax.axis_index(axis)
    gathered = jax.tree.map(lambda a: lax.all_gather(a, axis), part)
    state = jax.tree.map(lambda a, e: jnp.zeros_like(a) + jnp.asarray(e, a.dtype), part, identity)

    def one(hop, state):
        return combine(
            state, jax.tree.map(lambda a: lax.dynamic_index_in_dim(a, hop, 0, False), gathered)
        )

    return lax.fori_loop(0, place, one, state)


def layer_norm(values, gain, offset):
    center_mean = jnp.mean(values, axis=-1, keepdims=True)
    spread = jnp.mean(jnp.square(values - center_mean), axis=-1, keepdims=True)
    return (values - center_mean) * lax.rsqrt(spread + EPSILON) * gain + offset


def block_terms(inputs, b_in, c_in, decay):
    log_decay = jnp.log(decay)
    cumulative = jnp.cumsum(log_decay, axis=0)
    length = inputs.shape[0]
    sequence_indices = jnp.arange(length, dtype=jnp.int32)
    causal = sequence_indices[:, None] >= sequence_indices[None, :]
    log_gap = cumulative[:, None, :] - cumulative[None, :, :]
    weights = jnp.exp(jnp.where(causal[:, :, None], log_gap, -1e30))
    driven = inputs * (1.0 - decay)[:, :, None]
    affinity = jnp.dot(c_in, b_in.T, preferred_element_type=jnp.float32)
    within = jnp.einsum("tsh,shp->thp", affinity[:, :, None] * weights, driven, precision=HIGHEST)
    tail_decay = jnp.exp(cumulative[-1][None, :] - cumulative)
    end_state = jnp.einsum(
        "sh,shp,sn->hpn", tail_decay, driven, b_in.astype(jnp.float32), precision=HIGHEST
    )
    return (within, jnp.exp(cumulative), jnp.exp(cumulative[-1]), end_state)


def combine_states(earlier, later):
    return (earlier[0] * later[0], later[0][:, None, None] * earlier[1] + later[1])


def per_device(
    frames,
    segment_ids,
    ln_gain,
    ln_bias,
    qkv_weight,
    out_weight,
    out_bias,
    adapter,
    rms_gain,
    x_weight,
    bc_weight,
    decay,
    skip_gain,
):
    frame_count = frames.shape[0]
    margin = WINDOW
    tm_slot = lax.axis_index("tm")
    gathered = lax.all_gather(frames, "head", axis=1, tiled=True)
    normed = layer_norm(gathered.astype(jnp.float32), ln_gain, ln_bias).astype(jnp.bfloat16)
    queries = jnp.dot(normed, qkv_weight[0], preferred_element_type=jnp.float32).astype(
        jnp.bfloat16
    )
    keys_own = jnp.dot(normed, qkv_weight[1], preferred_element_type=jnp.float32).astype(
        jnp.bfloat16
    )
    values_own = jnp.dot(normed, qkv_weight[2], preferred_element_type=jnp.float32).astype(
        jnp.bfloat16
    )
    joined = jnp.concatenate([keys_own, values_own], axis=1)
    extended = with_halo(joined, (("tm", 0),), margin)
    head_width = keys_own.shape[1]
    keys_ext = extended[:, :head_width]
    values_ext = extended[:, head_width:]
    ids_pad = jnp.pad(segment_ids, (margin, margin), constant_values=-1)
    local_ids = lax.dynamic_slice_in_dim(
        ids_pad, tm_slot * frame_count, frame_count + 2 * margin, 0
    )
    heads_dev = queries.shape[1] // EHEAD_DIM
    qblock = math.gcd(frame_count, 512)
    span_rows = qblock + 2 * margin

    def attend(block_index):
        begin = block_index * qblock
        query_rows = queries.reshape(qblock, heads_dev, EHEAD_DIM)
        key_rows = keys_ext.reshape(span_rows, heads_dev, EHEAD_DIM)
        value_rows = values_ext.reshape(span_rows, heads_dev, EHEAD_DIM)
        query_ids = lax.dynamic_slice_in_dim(local_ids, begin + margin, qblock, 0)
        scores = jnp.einsum(
            "qhe,khe->hqk", query_rows, key_rows, preferred_element_type=jnp.float32
        ) * EHEAD_DIM ** (-0.5)
        allowed = query_ids[:, None] == local_ids[None, :]
        scores = jnp.where(allowed[None], scores, -1e30)
        peak = jnp.max(scores, axis=-1, keepdims=True)
        raised = jnp.exp(scores - peak)
        probs = (raised / jnp.sum(raised, axis=-1, keepdims=True)).astype(jnp.bfloat16)
        blended = jnp.einsum("hqk,khe->qhe", probs, value_rows, preferred_element_type=jnp.float32)
        return blended.astype(jnp.bfloat16).reshape(qblock, heads_dev * EHEAD_DIM)

    attended = lax.map(attend, jnp.arange(frame_count // qblock, dtype=jnp.int32)).reshape(
        frame_count, heads_dev * EHEAD_DIM
    )
    attention = jnp.dot(
        lax.all_gather(attended, "head", axis=1, tiled=True),
        out_weight,
        preferred_element_type=jnp.float32,
    )
    encoded = (frames.astype(jnp.float32) + attention + out_bias).astype(jnp.bfloat16)
    pooled = jnp.mean(
        encoded.astype(jnp.float32).reshape(frame_count // 4, 4, encoded.shape[1]), axis=1
    ).astype(jnp.bfloat16)
    partial_sum = jnp.dot(pooled, adapter, preferred_element_type=jnp.float32)
    projected = lax.psum(partial_sum, "head")
    scaled = (
        projected
        * lax.rsqrt(jnp.mean(jnp.square(projected), axis=1, keepdims=True) + EPSILON)
        * rms_gain
    ).astype(jnp.bfloat16)
    inputs = jax.nn.silu(jnp.dot(scaled, x_weight, preferred_element_type=jnp.float32)).astype(
        jnp.bfloat16
    )
    coupler_part = jax.nn.silu(
        jnp.dot(scaled, bc_weight, preferred_element_type=jnp.float32)
    ).astype(jnp.bfloat16)
    couplers = lax.all_gather(coupler_part, "head", axis=1, tiled=True)
    token_count = inputs.shape[0]
    state_heads = inputs.shape[1] // HDIM
    inputs_wide = inputs.astype(jnp.float32).reshape(token_count, state_heads, HDIM)
    c_rows = couplers[:, NSTATE:]
    within, growth, total_decay, end_state = block_terms(
        inputs_wide, couplers[:, :NSTATE], c_rows, decay
    )
    identity = (jnp.ones_like(total_decay), jnp.zeros_like(end_state))
    incoming = prefix((total_decay, end_state), "tm", combine_states, identity)
    from_state = jnp.einsum(
        "tn,hpn->thp", c_rows.astype(jnp.float32), incoming[1], precision=HIGHEST
    )
    result_rows = within + growth[:, :, None] * from_state + skip_gain[None, :, None] * inputs_wide
    mixed = result_rows.astype(jnp.bfloat16).reshape(token_count, state_heads * HDIM)
    return (encoded, mixed)


def solution(mesh):
    placed = (
        P("tm", "head"),
        P(),
        P(),
        P(),
        P(None, None, "head"),
        P(None, "head"),
        P("head"),
        P("head", None),
        P(),
        P(None, "head"),
        P(None, "head"),
        P("tm", "head"),
        P("head"),
    )
    return jax.shard_map(
        per_device,
        mesh=mesh,
        in_specs=placed,
        out_specs=(P("tm", "head"), P("tm", "head")),
        check_vma=False,
    )
```

profile of v0, /device:TPU:483, one launch (start us, length us, event | category | flops | bytes accessed | tf_op | source)
XLA Modules:
  0.0 432.9 jit_solution(7128152274875315925)
XLA Ops:
  7.3 29.6 %all_gather.19 = bf16[256,1280]{0,1:T(8,128)(2,1)S(1)} all-gather(bf16[256,160]{0,1:T(8,128)(2,1)} %param.15), channel_id=1, replica_groups=mesh['tm'=64,'head'=8] {'head'}, dimensions={1}, use_global_device_ids=true | all-gather | bytes 737280 | tf_op jit(solution)/shard_map/all_gather | solution.py:87
  38.4 8.7 %collective-permute-start.1 = (bf16[256,256]{0,1:T(8,128)(2,1)S(1)}, bf16[256,256]{0,1:T(8,128)(2,1)S(1)}, u32[]{:S(2)}, u32[]{:S(2)}) collective-permute-start(bf16[256,256]{0,1:T(8,128)(2,1)S(1)} %pad_maximum_fusion.1), channel_id=1, source_target_pairs={{8,0},{16,8},{24,16},{32,24},{40,32},{48,40},{56,48},{64,56},{72,6... | collective-permute-start | bytes 393224 | tf_op jit(solution)/shard_map/ppermute | solution.py:23
  47.1 1.3 collective-permute-start
  49.1 1.2 collective-permute-done
  52.2 29.1 %all_gather.20 = bf16[256,1024]{0,1:T(8,128)(2,1)S(1)} all-gather(bf16[256,128]{0,1:T(8,128)(2,1)S(1)} %bitcast.65), channel_id=1, replica_groups=mesh['tm'=64,'head'=8] {'head'}, dimensions={1}, use_global_device_ids=true | all-gather | bytes 589824 | tf_op jit(solution)/shard_map/all_gather | solution.py:132
  82.1 1.1 fusion.37
  83.6 103.0 %all-reduce.3.cloned.1.call-done = f32[64,2560]{1,0:T(8,128)} async-done(((f32[64,2560]{1,0:T(8,128)}), f32[64,2560]{1,0:T(8,128)}) %all-reduce.3.cloned.1.call-update) | async-done | bytes 655376 | tf_op jit(solution)/shard_map/psum | solution.py:141
  186.6 1.3 multiply_reduce_fusion
  188.0 1.4 multiply_convert_fusion.4
  189.4 28.0 %all_gather.21 = bf16[64,256]{0,1:T(8,128)(2,1)S(1)} all-gather(bf16[64,32]{0,1:T(8,128)(2,1)S(1)} %multiply_convert_fusion.4), channel_id=1, replica_groups=mesh['tm'=64,'head'=8] {'head'}, dimensions={1}, use_global_device_ids=true | all-gather | bytes 36864 | tf_op jit(solution)/shard_map/all_gather | solution.py:153
  219.2 71.0 %all-gather.1 = f32[64,1,5]{2,1,0:T(1,128)S(1)} all-gather(f32[1,1,5]{2,1,0:T(1,128)S(1)} %get-tuple-element.86), channel_id=1, replica_groups=mesh['tm'=64,'head'=8] {'tm'}, dimensions={0}, use_global_device_ids=true | all-gather | bytes 1300 | tf_op jit(solution)/shard_map/all_gather | solution.py:30
  290.4 67.9 %all-gather.4.cloned.1.call-done = f32[320,64,128]{2,1,0:T(8,128)} async-done(((f32[5,64,128]{2,1,0:T(8,128)}), f32[320,64,128]{2,1,0:T(8,128)}) %all-gather.4.cloned.1.call-update) | async-done | bytes 10485776 | tf_op jit(solution)/shard_map/all_gather | solution.py:30
  358.3 66.4 %while.3 = (s32[]{:T(128)}, f32[5,64,128]{2,1,0:T(8,128)S(1)}, s32[]{:T(128)}, f32[64,5]{1,0:T(8,128)S(1)}, f32[64,5,64,128]{3,2,1,0:T(8,128)}, /*index=5*/s32[]{:T(128)}, s32[]{:T(128)}, s32[]{:T(128)}) while((s32[]{:T(128)}, f32[5,64,128]{2,1,0:T(8,128)S(1)}, s32[]{:T(128)}, f32[64,5]{1,0:T(8,128)S(1)}, f32[64,5,64,128]{3,2,1,0:T(8,128)}, ...), condition=%wide.region_9.10_spmd, body=%wide.region_8.9_spmd.sunk | while | flops 81925 | bytes 491715 | solution.py:38
  358.3 1.0 bitcast_add_fusion.2
  359.4 1.0 bitcast_add_fusion.2
  360.5 1.0 bitcast_add_fusion.2
  361.5 1.0 bitcast_add_fusion.2
  362.6 1.0 bitcast_add_fusion.2
  364.7 1.0 bitcast_add_fusion.2
  365.7 1.0 bitcast_add_fusion.2
  366.8 1.0 bitcast_add_fusion.2
  367.8 1.0 bitcast_add_fusion.2
  368.9 1.0 bitcast_add_fusion.2
  369.9 1.0 bitcast_add_fusion.2
  371.0 1.0 bitcast_add_fusion.2
  372.0 1.0 bitcast_add_fusion.2
  374.1 1.0 bitcast_add_fusion.2
  375.2 1.0 bitcast_add_fusion.2
  376.3 1.0 bitcast_add_fusion.2
  377.3 1.0 bitcast_add_fusion.2
  378.4 1.0 bitcast_add_fusion.2
  379.4 1.0 bitcast_add_fusion.2
  (180 shorter events, 53.7 us)
Async XLA Ops:
  7.2 210.2 %copy-start = (bf16[2560,320]{0,1:T(8,128)(2,1)S(1)}, bf16[2560,320]{0,1:T(8,128)(2,1)}, u32[]{:S(2)}) copy-start(bf16[2560,320]{0,1:T(8,128)(2,1)} %param.24) | copy-start | bytes 4915204
  7.2 30.1 %copy-start.9 = (f32[1280]{0:T(1024)S(1)}, f32[1280]{0:T(1024)}, u32[]{:S(2)}) copy-start(f32[1280]{0:T(1024)} %param.18) | copy-start | bytes 15364
  7.2 30.1 %copy-start.10 = (f32[1280]{0:T(1024)S(1)}, f32[1280]{0:T(1024)}, u32[]{:S(2)}) copy-start(f32[1280]{0:T(1024)} %param.17) | copy-start | bytes 15364
  7.2 30.5 %copy-start.14 = (bf16[3,1280,128]{2,1,0:T(8,128)(2,1)S(1)}, bf16[3,1280,128]{2,1,0:T(8,128)(2,1)}, u32[]{:S(2)}) copy-start(bf16[3,1280,128]{2,1,0:T(8,128)(2,1)} %param.19) | copy-start | bytes 2949124
  7.2 179.4 %all-reduce.3.cloned.1.call-start = ((), (), s32[]{:S(2)}) async-start(), calls=%async_computation | async-start | bytes 1310720 | tf_op jit(solution)/shard_map/psum | solution.py:141
  38.1 10.7 %copy-start.6 = (s32[16384]{0:T(1024)S(1)}, s32[16384]{0:T(1024)}, u32[]{:S(2)}) copy-start(s32[16384]{0:T(1024)} %param.16) | copy-start | bytes 196612
  38.4 10.7 %collective-permute-start.1 = (bf16[256,256]{0,1:T(8,128)(2,1)S(1)}, bf16[256,256]{0,1:T(8,128)(2,1)S(1)}, u32[]{:S(2)}, u32[]{:S(2)}) collective-permute-start(bf16[256,256]{0,1:T(8,128)(2,1)S(1)} %pad_maximum_fusion.1), channel_id=1, source_target_pairs={{8,0},{16,8},{24,16},{32,24},{40,32},{48,40},{56,48},{64,56},{72,6... | collective-permute-start | bytes 393224 | tf_op jit(solution)/shard_map/ppermute | solution.py:23
  47.1 3.2 collective-permute-start
  51.2 30.2 %copy-start.4 = (bf16[1024,160]{0,1:T(8,128)(2,1)S(1)}, bf16[1024,160]{0,1:T(8,128)(2,1)}, u32[]{:S(2)}) copy-start(bf16[1024,160]{0,1:T(8,128)(2,1)} %param.20) | copy-start | bytes 983044
  51.2 30.2 %copy-start.5 = (bf16[256,160]{0,1:T(8,128)(2,1)S(1)}, bf16[256,160]{0,1:T(8,128)(2,1)}, u32[]{:S(2)}) copy-start(bf16[256,160]{0,1:T(8,128)(2,1)} %param.15) | copy-start | bytes 245764
  51.2 30.2 %copy-start.12 = (f32[160]{0:T(256)S(1)}, f32[160]{0:T(256)}, u32[]{:S(2)}) copy-start(f32[160]{0:T(256)} %param.21) | copy-start | bytes 1924
  52.2 29.8 %copy-start.2 = (bf16[160,2560]{1,0:T(8,128)(2,1)S(1)}, bf16[160,2560]{1,0:T(8,128)(2,1)}, u32[]{:S(2)}) copy-start(bf16[160,2560]{1,0:T(8,128)(2,1)} %param.22) | copy-start | bytes 2457604
  81.7 1.6 copy-start.3
  81.8 1.5 copy-start.11
  82.1 105.9 %copy-start.7 = (bf16[2560,32]{0,1:T(8,128)(2,1)S(1)}, bf16[2560,32]{0,1:T(8,128)(2,1)}, u32[]{:S(2)}) copy-start(bf16[2560,32]{0,1:T(8,128)(2,1)} %param.25) | copy-start | bytes 491524
  82.1 105.9 %copy-start.8 = (f32[2560]{0:T(1024)S(1)}, f32[2560]{0:T(1024)}, u32[]{:S(2)}) copy-start(f32[2560]{0:T(1024)} %param.23) | copy-start | bytes 30724
  83.2 275.1 %all-gather.4.cloned.1.call-start = ((), (), s32[]{:S(2)}) async-start(), calls=%async_computation.1 | async-start | bytes 10649600 | tf_op jit(solution)/shard_map/all_gather | solution.py:30
  186.6 30.8 %copy-start.1 = (f32[64,2560]{1,0:T(8,128)S(1)}, f32[64,2560]{1,0:T(8,128)}, u32[]{:S(2)}) copy-start(f32[64,2560]{1,0:T(8,128)} %all-reduce.3.cloned.1.call-done) | copy-start | bytes 1966084
  358.3 66.6 %copy-start.13 = (f32[5]{0:T(128)S(1)}, f32[5]{0:T(128)}, u32[]{:S(2)}) copy-start(f32[5]{0:T(128)} %param.27) | copy-start | bytes 64
Sparse Core Ops, SparseCore 0:
  83.3 103.2 all-reduce.2
  219.2 139.0 all-gather.3
where the time goes:
time: 435 us; the launch traced here: 433 us
  waiting for transfers between devices  172 us (40%)
  blocking collectives  158 us (36%)
  other arithmetic  66.5 us (15%)
  between operations  14.4 us (3%)
  starting transfers between devices  10.1 us (2%)
  matrix products  7.89 us (2%)
    psum x1, waiting for transfers between devices, per_device(): projected = lax.psum(partial_sum, 'head')  103 us
    all_gather x1, blocking collectives, prefix(): gathered = jax.tree.map(lambda a: lax.all_gather(a, axis), part)  71 us
    all_gather x1, waiting for transfers between devices, prefix(): gathered = jax.tree.map(lambda a: lax.all_gather(a, axis), part)  67.9 us
    add x63, other arithmetic, combine_states(): later[0][:, None, None] * earlier[1] + later[1]  63.8 us
    all_gather x1, blocking collectives, per_device(): gathered = lax.all_gather(frames, 'head', axis=1, tiled=True)  29.6 us
    all_gather x1, blocking collectives, per_device(): lax.all_gather(attended, 'head', axis=1, tiled=True)  29.1 us
    all_gather x1, blocking collectives, per_device(): couplers = lax.all_gather(coupler_part, 'head', axis=1, tiled=True)  28 us
  transfers between devices with their start and end apart: 4, of which 3 were waited for; matrix products, arithmetic and copies ran while one was open for 0% of the time, Pallas kernels for 0%

commit v1 on v0

--- a/solution.py
+++ b/solution.py
@@ -84,7 +84,9 @@
     frame_count = frames.shape[0]
     margin = WINDOW
     tm_slot = lax.axis_index("tm")
-    gathered = lax.all_gather(frames, "head", axis=1, tiled=True)
+    gathered = jnp.concatenate(
+        lax.all_to_all(jnp.stack([frames] * lax.axis_size("head")), "head", 0, 0), axis=1
+    )
     normed = layer_norm(gathered.astype(jnp.float32), ln_gain, ln_bias).astype(jnp.bfloat16)
     queries = jnp.dot(normed, qkv_weight[0], preferred_element_type=jnp.float32).astype(
         jnp.bfloat16

time: 435 us -> 417 us (0.959)
  the two profiles are of different devices: /device:TPU:483 before, /device:TPU:487 now
where the time goes in v1:
time: 417 us; the launch traced here: 415 us
  waiting for transfers between devices  181 us (43%)
  blocking collectives  128 us (31%)
  other arithmetic  66.5 us (16%)
  between operations  14.4 us (3%)
  starting transfers between devices  10.9 us (3%)
  matrix products  7.86 us (2%)
  local copies, waits for them, and re-layouts  4.25 us (1%)
    psum x1, waiting for transfers between devices, per_device(): projected = lax.psum(partial_sum, 'head')  101 us
    all_gather x1, blocking collectives, prefix(): gathered = jax.tree.map(lambda a: lax.all_gather(a, axis), part)  70.7 us
    all_gather x1, waiting for transfers between devices, prefix(): gathered = jax.tree.map(lambda a: lax.all_gather(a, axis), part)  68.4 us
    add x63, other arithmetic, combine_states(): later[0][:, None, None] * earlier[1] + later[1]  63.8 us
    all_gather x1, blocking collectives, per_device(): lax.all_gather(attended, 'head', axis=1, tiled=True)  29.5 us
    all_gather x1, blocking collectives, per_device(): couplers = lax.all_gather(coupler_part, 'head', axis=1, tiled=True)  27.8 us
    all_to_all x1, waiting for transfers between devices, per_device(): lax.all_to_all(jnp.stack([frames] * lax.axis_size('head')), 'head', 0, 0)  9.97 us
  transfers between devices with their start and end apart: 5, of which 4 were waited for; matrix products, arithmetic and copies ran while one was open for 0% of the time, Pallas kernels for 0%

profile of v1, /device:TPU:487, one launch (start us, length us, event | category | flops | bytes accessed | tf_op | source)
XLA Modules:
  0.0 414.9 jit_solution(17677580264237363090)
XLA Ops:
  7.2 1.9 stack.2
  9.1 6.9 %all-to-all-start = ((bf16[8,256,160]{1,2,0:T(8,128)(2,1)}), bf16[8,256,160]{1,2,0:T(8,128)(2,1)S(1)}, u32[]{:S(2)}, u32[]{:S(2)}) async-start(bf16[8,256,160]{1,2,0:T(8,128)(2,1)} %stack.2), calls=%async_computation | async-start | bytes 1310720 | tf_op jit(solution)/shard_map/all_to_all | solution.py:88
  16.5 10.0 %all-to-all-done = bf16[8,256,160]{1,2,0:T(8,128)(2,1)S(1)} async-done(((bf16[8,256,160]{1,2,0:T(8,128)(2,1)}), bf16[8,256,160]{1,2,0:T(8,128)(2,1)S(1)}, u32[]{:S(2)}, u32[]{:S(2)}) %all-to-all-start) | async-done | bytes 655392 | tf_op jit(solution)/shard_map/all_to_all | solution.py:88
  28.0 2.7 collective-permute-start.1
  30.7 1.3 collective-permute-start
  32.3 1.6 collective-permute-done
  35.8 29.5 %all_gather.16 = bf16[256,1024]{0,1:T(8,128)(2,1)S(1)} all-gather(bf16[256,128]{0,1:T(8,128)(2,1)S(1)} %bitcast.71), channel_id=1, replica_groups=mesh['tm'=64,'head'=8] {'head'}, dimensions={1}, use_global_device_ids=true | all-gather | bytes 589824 | tf_op jit(solution)/shard_map/all_gather | solution.py:134
  66.0 1.1 fusion.37
  67.5 101.0 %all-reduce.3.cloned.1.call-done = f32[64,2560]{1,0:T(8,128)} async-done(((f32[64,2560]{1,0:T(8,128)}), f32[64,2560]{1,0:T(8,128)}) %all-reduce.3.cloned.1.call-update) | async-done | bytes 655376 | tf_op jit(solution)/shard_map/psum | solution.py:143
  168.5 1.3 multiply_reduce_fusion
  169.8 1.4 multiply_convert_fusion.4
  171.2 27.8 %all_gather.17 = bf16[64,256]{0,1:T(8,128)(2,1)S(1)} all-gather(bf16[64,32]{0,1:T(8,128)(2,1)S(1)} %multiply_convert_fusion.4), channel_id=1, replica_groups=mesh['tm'=64,'head'=8] {'head'}, dimensions={1}, use_global_device_ids=true | all-gather | bytes 36864 | tf_op jit(solution)/shard_map/all_gather | solution.py:155
  200.9 70.7 %all-gather.1 = f32[64,1,5]{2,1,0:T(1,128)S(1)} all-gather(f32[1,1,5]{2,1,0:T(1,128)S(1)} %get-tuple-element.86), channel_id=1, replica_groups=mesh['tm'=64,'head'=8] {'tm'}, dimensions={0}, use_global_device_ids=true | all-gather | bytes 1300 | tf_op jit(solution)/shard_map/all_gather | solution.py:30
  271.8 68.4 %all-gather.4.cloned.1.call-done = f32[320,64,128]{2,1,0:T(8,128)} async-done(((f32[5,64,128]{2,1,0:T(8,128)}), f32[320,64,128]{2,1,0:T(8,128)}) %all-gather.4.cloned.1.call-update) | async-done | bytes 10485776 | tf_op jit(solution)/shard_map/all_gather | solution.py:30
  340.2 66.4 %while.3 = (s32[]{:T(128)}, f32[5,64,128]{2,1,0:T(8,128)S(1)}, s32[]{:T(128)}, f32[64,5]{1,0:T(8,128)S(1)}, f32[64,5,64,128]{3,2,1,0:T(8,128)}, /*index=5*/s32[]{:T(128)}, s32[]{:T(128)}, s32[]{:T(128)}) while((s32[]{:T(128)}, f32[5,64,128]{2,1,0:T(8,128)S(1)}, s32[]{:T(128)}, f32[64,5]{1,0:T(8,128)S(1)}, f32[64,5,64,128]{3,2,1,0:T(8,128)}, ...), condition=%wide.region_9.10_spmd, body=%wide.region_8.9_spmd.sunk | while | flops 81925 | bytes 491715 | solution.py:38
  340.3 1.0 bitcast_add_fusion.2
  341.3 1.0 bitcast_add_fusion.2
  342.4 1.0 bitcast_add_fusion.2
  343.4 1.0 bitcast_add_fusion.2
  344.5 1.0 bitcast_add_fusion.2
  346.6 1.0 bitcast_add_fusion.2
  347.6 1.0 bitcast_add_fusion.2
  348.7 1.0 bitcast_add_fusion.2
  349.8 1.0 bitcast_add_fusion.2
  350.8 1.0 bitcast_add_fusion.2
  351.9 1.0 bitcast_add_fusion.2
  352.9 1.0 bitcast_add_fusion.2
  354.0 1.0 bitcast_add_fusion.2
  355.0 1.0 bitcast_add_fusion.2
  357.1 1.0 bitcast_add_fusion.2
  358.2 1.0 bitcast_add_fusion.2
  359.2 1.0 bitcast_add_fusion.2
  (184 shorter events, 55.8 us)
Async XLA Ops:
  7.2 191.9 %copy-start = (bf16[2560,320]{0,1:T(8,128)(2,1)S(1)}, bf16[2560,320]{0,1:T(8,128)(2,1)}, u32[]{:S(2)}) copy-start(bf16[2560,320]{0,1:T(8,128)(2,1)} %param.24) | copy-start | bytes 4915204
  7.2 8.8 %copy-start.9 = (f32[1280]{0:T(1024)S(1)}, f32[1280]{0:T(1024)}, u32[]{:S(2)}) copy-start(f32[1280]{0:T(1024)} %param.17) | copy-start | bytes 15364
  7.2 8.9 %copy-start.10 = (f32[1280]{0:T(1024)S(1)}, f32[1280]{0:T(1024)}, u32[]{:S(2)}) copy-start(f32[1280]{0:T(1024)} %param.18) | copy-start | bytes 15364
  7.2 8.9 %copy-start.6 = (s32[16384]{0:T(1024)S(1)}, s32[16384]{0:T(1024)}, u32[]{:S(2)}) copy-start(s32[16384]{0:T(1024)} %param.16) | copy-start | bytes 196612
  9.1 17.3 %all-to-all-start = ((bf16[8,256,160]{1,2,0:T(8,128)(2,1)}), bf16[8,256,160]{1,2,0:T(8,128)(2,1)S(1)}, u32[]{:S(2)}, u32[]{:S(2)}) async-start(bf16[8,256,160]{1,2,0:T(8,128)(2,1)} %stack.2), calls=%async_computation | async-start | bytes 1310720 | tf_op jit(solution)/shard_map/all_to_all | solution.py:88
  16.0 11.3 %copy-start.14 = (bf16[3,1280,128]{2,1,0:T(8,128)(2,1)S(1)}, bf16[3,1280,128]{2,1,0:T(8,128)(2,1)}, u32[]{:S(2)}) copy-start(bf16[3,1280,128]{2,1,0:T(8,128)(2,1)} %param.19) | copy-start | bytes 2949124
  16.0 152.5 %all-reduce.3.cloned.1.call-start = ((), (), s32[]{:S(2)}) async-start(), calls=%async_computation.1 | async-start | bytes 1310720 | tf_op jit(solution)/shard_map/psum | solution.py:143
  28.0 4.3 %collective-permute-start.1 = (bf16[256,256]{0,1:T(8,128)(2,1)S(1)}, bf16[256,256]{0,1:T(8,128)(2,1)S(1)}, u32[]{:S(2)}, u32[]{:S(2)}) collective-permute-start(bf16[256,256]{0,1:T(8,128)(2,1)S(1)} %pad_maximum_fusion.1), channel_id=1, source_target_pairs={{8,0},{16,8},{24,16},{32,24},{40,32},{48,40},{56,48},{64,56},{72,6... | collective-permute-start | bytes 393224 | tf_op jit(solution)/shard_map/ppermute | solution.py:23
  30.7 3.2 collective-permute-start
  34.8 30.5 %copy-start.4 = (bf16[1024,160]{0,1:T(8,128)(2,1)S(1)}, bf16[1024,160]{0,1:T(8,128)(2,1)}, u32[]{:S(2)}) copy-start(bf16[1024,160]{0,1:T(8,128)(2,1)} %param.20) | copy-start | bytes 983044
  34.8 30.5 %copy-start.5 = (bf16[256,160]{0,1:T(8,128)(2,1)S(1)}, bf16[256,160]{0,1:T(8,128)(2,1)}, u32[]{:S(2)}) copy-start(bf16[256,160]{0,1:T(8,128)(2,1)} %param.15) | copy-start | bytes 245764
  34.8 30.5 %copy-start.12 = (f32[160]{0:T(256)S(1)}, f32[160]{0:T(256)}, u32[]{:S(2)}) copy-start(f32[160]{0:T(256)} %param.21) | copy-start | bytes 1924
  35.8 30.2 %copy-start.2 = (bf16[160,2560]{1,0:T(8,128)(2,1)S(1)}, bf16[160,2560]{1,0:T(8,128)(2,1)}, u32[]{:S(2)}) copy-start(bf16[160,2560]{1,0:T(8,128)(2,1)} %param.22) | copy-start | bytes 2457604
  65.6 1.5 copy-start.3
  65.7 1.5 copy-start.11
  66.0 103.8 %copy-start.7 = (bf16[2560,32]{0,1:T(8,128)(2,1)S(1)}, bf16[2560,32]{0,1:T(8,128)(2,1)}, u32[]{:S(2)}) copy-start(bf16[2560,32]{0,1:T(8,128)(2,1)} %param.25) | copy-start | bytes 491524
  66.0 103.8 %copy-start.8 = (f32[2560]{0:T(1024)S(1)}, f32[2560]{0:T(1024)}, u32[]{:S(2)}) copy-start(f32[2560]{0:T(1024)} %param.23) | copy-start | bytes 30724
  67.1 273.1 %all-gather.4.cloned.1.call-start = ((), (), s32[]{:S(2)}) async-start(), calls=%async_computation.2 | async-start | bytes 10649600 | tf_op jit(solution)/shard_map/all_gather | solution.py:30
  168.5 30.6 %copy-start.1 = (f32[64,2560]{1,0:T(8,128)S(1)}, f32[64,2560]{1,0:T(8,128)}, u32[]{:S(2)}) copy-start(f32[64,2560]{1,0:T(8,128)} %all-reduce.3.cloned.1.call-done) | copy-start | bytes 1966084
  340.2 66.6 %copy-start.13 = (f32[5]{0:T(128)S(1)}, f32[5]{0:T(128)}, u32[]{:S(2)}) copy-start(f32[5]{0:T(128)} %param.27) | copy-start | bytes 64
Sparse Core Ops, SparseCore 0:
  67.2 101.2 all-reduce.2
  200.9 139.3 all-gather.3
